TPU v7x, 32 devices: a whole 2x2x4 slice. The times are simulated.
32 devices in a mesh: wide: 8 (over z, y), narrow: 4 (over x, core).
Axes of the slice: x: 2, y: 2, z: 4, core: 2. Of those that a mesh axis runs over, the one named last changes fastest.
Arguments:
- media_feats: bfloat16 [8, 2048, 1536], P('wide', 'narrow'), may hold values from -6 to 6
- latents: bfloat16 [8, 64, 1536], P('wide', 'narrow'), may hold values from -6 to 6
- frame_counts: int32 [8], P('wide'), may hold values from 1 to 8, as said below
- media_mask: int32 [8, 2048], P('wide'), may hold values 0 or 1
- time_embed: bfloat16 [8, 1536], replicated, may hold values from -3 to 3
- media_gain: float32 [1536], replicated, may hold values from 0.1 to 1.9
- media_bias: float32 [1536], replicated, may hold values from -1.75 to 1.75
- latent_gain: float32 [1536], replicated, may hold values from 0.1 to 1.9
- latent_bias: float32 [1536], replicated, may hold values from -1.75 to 1.75
- ffn_gain: float32 [1536], replicated, may hold values from 0.1 to 1.9
- ffn_bias: float32 [1536], replicated, may hold values from -1.75 to 1.75
- query_weight: bfloat16 [1536, 1536], P('wide', 'narrow'), may hold values from -0.3125 to 0.3125
- keyval_weight: bfloat16 [1536, 2, 1536], P('wide', None, 'narrow'), may hold values from -0.15625 to 0.15625
- output_weight: bfloat16 [1536, 1536], P('narrow', 'wide'), may hold values from -0.625 to 0.625
- up_weight: bfloat16 [1536, 6144], P(None, 'narrow'), may hold values from -0.15625 to 0.15625
- down_weight: bfloat16 [6144, 1536], P('narrow'), may hold values from -0.078125 to 0.078125
- cotangent: bfloat16 [8, 64, 1536], P('wide', 'narrow'), may hold values from -6 to 6
Outputs:
- out_latents: bfloat16 [8, 64, 1536], P('wide', 'narrow')
- grad_media: bfloat16 [8, 2048, 1536], P('wide', 'narrow')
- grad_latents: bfloat16 [8, 64, 1536], P('wide', 'narrow')
- grad_time_embed: float32 [8, 1536], P(None, ('wide', 'narrow'))
- grad_media_gain: float32 [1536], P(('wide', 'narrow'))
- grad_media_bias: float32 [1536], P(('wide', 'narrow'))
- grad_latent_gain: float32 [1536], P(('wide', 'narrow'))
- grad_latent_bias: float32 [1536], P(('wide', 'narrow'))
- grad_ffn_gain: float32 [1536], P(('wide', 'narrow'))
- grad_ffn_bias: float32 [1536], P(('wide', 'narrow'))
- grad_query_weight: float32 [1536, 1536], P('wide', 'narrow')
- grad_keyval_weight: float32 [1536, 2, 1536], P('wide', None, 'narrow')
- grad_output_weight: float32 [1536, 1536], P('narrow', 'wide')
- grad_up_weight: float32 [1536, 6144], P('wide', 'narrow')
- grad_down_weight: float32 [6144, 1536], P('narrow', 'wide')
Inputs may be any that keep to these rules, and one draw needn't show every extreme that they name: `frame_counts`: frames of each item; some item has exactly 8.
All inputs are finite; a program needn't handle non-finite values. No bound on the sum of `media_mask` on one device may be relied on, other than what follows from the above.
Results may differ from a plain program's by a relative error of at most 0.02.
Values may be sent and summed in bfloat16 or wider, within the bound.
A program may use at most 128 MiB of HBM per device.

v0:
```python
import math
import jax
import jax.numpy as jnp
from jax import lax
from jax.sharding import PartitionSpec as P

HEADS = 16
HEAD_DIM = 96
FRAMES_MAX = 8
PATCHES = 256
EPS = 1e-05
ENT_COEF = 4.0
HIGH = lax.Precision.HIGHEST


def norm_forward(values, norm_gain, norm_bias):
    row_mean = jnp.mean(values, axis=-1, keepdims=True)
    centered = values - row_mean
    inv_std = lax.rsqrt(jnp.mean(centered * centered, axis=-1, keepdims=True) + EPS)
    normed = centered * inv_std
    return (normed * norm_gain + norm_bias, normed, inv_std)


def norm_backward(grad_out, normed, inv_std, norm_gain):
    scaled = grad_out * norm_gain
    grad_in = inv_std * (
        scaled
        - jnp.mean(scaled, axis=-1, keepdims=True)
        - normed * jnp.mean(scaled * normed, axis=-1, keepdims=True)
    )
    return (grad_in, jnp.sum(grad_out * normed, axis=0), jnp.sum(grad_out, axis=0))


def gelu_slope(pre_act):
    cdf_part = 0.5 * (1.0 + lax.erf(pre_act * (1.0 / math.sqrt(2.0))))
    density = jnp.exp(-0.5 * pre_act * pre_act) * (1.0 / math.sqrt(2.0 * math.pi))
    return cdf_part + pre_act * density


def body(
    media_feats,
    latents,
    frame_counts,
    media_mask,
    time_embed,
    media_gain,
    media_bias,
    latent_gain,
    latent_bias,
    ffn_gain,
    ffn_bias,
    query_weight,
    keyval_weight,
    output_weight,
    up_weight,
    down_weight,
    cotangent,
):
    item_count = media_feats.shape[0]
    own_media = media_feats.shape[1]
    width = media_feats.shape[2]
    own_latent = latents.shape[1]
    narrow_size = lax.axis_size("narrow")
    narrow_pos = lax.axis_index("narrow")
    media_total = own_media * narrow_size
    latent_total = own_latent * narrow_size
    head_local = HEADS // narrow_size
    cols = head_local * HEAD_DIM
    key_total = media_total + latent_total
    all_ids = jnp.arange(media_total, dtype=jnp.int32) // PATCHES
    valid_tok = (all_ids[None, :] < frame_counts[:, None]) & (media_mask > 0)
    local_count = jnp.sum(valid_tok.astype(jnp.float32)) + float(item_count * latent_total)
    total_count = lax.psum(local_count, "wide")
    all_items = item_count * lax.axis_size("wide")
    ent_weight = ENT_COEF * float(all_items * media_total) / total_count
    query_own, keyval_own, output_own = (
        lax.all_gather(query_weight, "wide", axis=0, tiled=True),
        lax.all_gather(keyval_weight, "wide", axis=0, tiled=True),
        lax.all_gather(output_weight, "wide", axis=1, tiled=True),
    )
    query_full, keyval_full = (
        lax.all_gather(query_own, "narrow", axis=1, tiled=True),
        lax.all_gather(keyval_own, "narrow", axis=2, tiled=True),
    )
    keyval_flat = keyval_own.reshape(width, 2 * cols)
    own_ids = (narrow_pos * own_media + jnp.arange(own_media, dtype=jnp.int32)) // PATCHES
    frame_onehot = own_ids[:, None] == jnp.arange(FRAMES_MAX, dtype=jnp.int32)[None, :]
    time_rows = jnp.dot(
        frame_onehot.astype(jnp.bfloat16), time_embed, preferred_element_type=jnp.float32
    )
    score_scale = HEAD_DIM ** (-0.5)

    def item_step(carry, item):
        (
            down_acc,
            up_acc,
            output_acc,
            keyval_acc,
            query_acc,
            mg_acc,
            mb_acc,
            lg_acc,
            lb_acc,
            fg_acc,
            fb_acc,
            time_acc,
        ) = carry
        media_one, latent_one, valid_one, cot_one = item
        media_nf, media_hat, media_istd = norm_forward(
            media_one.astype(jnp.float32) + time_rows, media_gain, media_bias
        )
        latent_f32 = latent_one.astype(jnp.float32)
        latent_nf, latent_hat, latent_istd = norm_forward(latent_f32, latent_gain, latent_bias)
        media_all, latent_all = (
            lax.all_gather(media_nf.astype(jnp.bfloat16), "narrow", axis=0, tiled=True),
            lax.all_gather(latent_nf.astype(jnp.bfloat16), "narrow", axis=0, tiled=True),
        )
        keys_in = jnp.concatenate([media_all, latent_all], axis=0)
        query_act = jnp.dot(latent_all, query_own, preferred_element_type=jnp.float32).astype(
            jnp.bfloat16
        )
        key_vals = jnp.dot(keys_in, keyval_flat, preferred_element_type=jnp.float32).astype(
            jnp.bfloat16
        )
        query_heads = query_act.reshape(latent_total, head_local, HEAD_DIM)
        key_heads = key_vals[:, :cols].reshape(key_total, head_local, HEAD_DIM)
        value_heads = key_vals[:, cols:].reshape(key_total, head_local, HEAD_DIM)
        key_valid = jnp.concatenate([valid_one, jnp.ones((latent_total,), dtype=bool)])
        scores = (
            jnp.einsum("lhd,khd->hlk", query_heads, key_heads, preferred_element_type=jnp.float32)
            * score_scale
        )
        open_keys = key_valid[None, None, :]
        masked = jnp.where(open_keys, scores, -1e30)
        row_top = jnp.max(masked, axis=-1)
        expo = jnp.exp(masked - row_top[..., None])
        prob_all = expo / jnp.sum(expo, axis=-1)[..., None]
        prob_low = prob_all.astype(jnp.bfloat16)
        plain_scores = jnp.where(open_keys, scores, 0.0)
        mean_score = jnp.sum(prob_all * plain_scores, axis=-1)
        attn_out = jnp.einsum(
            "hlk,khd->lhd", prob_low, value_heads, preferred_element_type=jnp.float32
        ).reshape(latent_total, cols)
        attn_low = attn_out.astype(jnp.bfloat16)
        branch_part = jnp.dot(attn_low, output_own, preferred_element_type=jnp.float32)
        branch_own = lax.psum_scatter(
            branch_part.astype(jnp.bfloat16), "narrow", scatter_dimension=0, tiled=True
        ).astype(jnp.float32)
        latent_mid = latent_f32 + branch_own
        hidden_f, hidden_hat, hidden_istd = norm_forward(latent_mid, ffn_gain, ffn_bias)
        hidden_all, cot_all = (
            lax.all_gather(hidden_f.astype(jnp.bfloat16), "narrow", axis=0, tiled=True),
            lax.all_gather(cot_one, "narrow", axis=0, tiled=True),
        )
        pre_act = jnp.dot(hidden_all, up_weight, preferred_element_type=jnp.float32)
        act_low = jax.nn.gelu(pre_act, approximate=False).astype(jnp.bfloat16)
        ffn_part = jnp.dot(act_low, down_weight, preferred_element_type=jnp.float32)
        ffn_own = lax.psum_scatter(
            ffn_part.astype(jnp.bfloat16), "narrow", scatter_dimension=0, tiled=True
        ).astype(jnp.float32)
        out_one = (latent_mid + ffn_own).astype(jnp.bfloat16)
        down_acc = down_acc + jnp.einsum(
            "lf,ld->fd", act_low, cot_all, preferred_element_type=jnp.float32
        )
        grad_act = jnp.einsum("ld,fd->lf", cot_all, down_weight, preferred_element_type=jnp.float32)
        grad_pre = (grad_act * gelu_slope(pre_act)).astype(jnp.bfloat16)
        up_acc = up_acc + jnp.einsum(
            "ld,lf->df", hidden_all, grad_pre, preferred_element_type=jnp.float32
        )
        hidden_part = jnp.einsum(
            "lf,df->ld", grad_pre, up_weight, preferred_element_type=jnp.float32
        )
        grad_hidden = lax.psum_scatter(
            hidden_part.astype(jnp.bfloat16), "narrow", scatter_dimension=0, tiled=True
        ).astype(jnp.float32)
        grad_norm, fg_part, fb_part = norm_backward(grad_hidden, hidden_hat, hidden_istd, ffn_gain)
        grad_mid = cot_one.astype(jnp.float32) + grad_norm
        grad_branch_all = lax.all_gather(
            grad_mid.astype(jnp.bfloat16), "narrow", axis=0, tiled=True
        )
        output_acc = output_acc + jnp.einsum(
            "lc,ld->cd", attn_low, grad_branch_all, preferred_element_type=jnp.float32
        )
        grad_attn = jnp.einsum(
            "ld,cd->lc", grad_branch_all, output_own, preferred_element_type=jnp.float32
        ).astype(jnp.bfloat16)
        row_dots = jnp.sum(
            (grad_attn.astype(jnp.float32) * attn_out).reshape(latent_total, head_local, HEAD_DIM),
            axis=-1,
        )
        shift_rows = (jnp.transpose(row_dots, (1, 0)) - ent_weight * mean_score)[..., None]
        grad_heads = grad_attn.reshape(latent_total, head_local, HEAD_DIM)
        grad_prob = jnp.einsum(
            "lhd,khd->hlk", grad_heads, value_heads, preferred_element_type=jnp.float32
        )
        grad_scores = (prob_all * (grad_prob - ent_weight * plain_scores - shift_rows)).astype(
            jnp.bfloat16
        )
        grad_values = jnp.einsum(
            "hlk,lhd->khd", prob_low, grad_heads, preferred_element_type=jnp.float32
        ).reshape(key_total, cols)
        grad_keys = (
            jnp.einsum(
                "hlk,lhd->khd", grad_scores, query_heads, preferred_element_type=jnp.float32
            ).reshape(key_total, cols)
            * score_scale
        )
        grad_query = (
            jnp.einsum(
                "hlk,khd->lhd", grad_scores, key_heads, preferred_element_type=jnp.float32
            ).reshape(latent_total, cols)
            * score_scale
        ).astype(jnp.bfloat16)
        grad_pairs = jnp.concatenate([grad_keys, grad_values], axis=-1).astype(jnp.bfloat16)
        keyval_acc = keyval_acc + jnp.einsum(
            "kd,ke->de", keys_in, grad_pairs, preferred_element_type=jnp.float32
        )
        query_acc = query_acc + jnp.einsum(
            "ld,lc->dc", latent_all, grad_query, preferred_element_type=jnp.float32
        )
        media_pairs = grad_pairs[:media_total].reshape(media_total, 2, cols)
        latent_pairs = jnp.concatenate(
            [
                grad_pairs[media_total:].reshape(latent_total, 2, cols),
                grad_query.reshape(latent_total, 1, cols),
            ],
            axis=1,
        )
        media_back, latent_back = (
            lax.all_to_all(media_pairs, "narrow", split_axis=0, concat_axis=2, tiled=True),
            lax.all_to_all(latent_pairs, "narrow", split_axis=0, concat_axis=2, tiled=True),
        )
        grad_media_rows = jnp.einsum(
            "rsc,dsc->rd", media_back, keyval_full, preferred_element_type=jnp.float32
        )
        grad_latent_normed = jnp.einsum(
            "rsc,dsc->rd", latent_back[:, :2], keyval_full, preferred_element_type=jnp.float32
        ) + jnp.einsum(
            "rc,dc->rd", latent_back[:, 2], query_full, preferred_element_type=jnp.float32
        )
        grad_media_in, mg_part, mb_part = norm_backward(
            grad_media_rows, media_hat, media_istd, media_gain
        )
        time_acc = time_acc + jnp.einsum(
            "mf,md->fd", frame_onehot.astype(jnp.float32), grad_media_in, precision=HIGH
        )
        grad_latent_in, lg_part, lb_part = norm_backward(
            grad_latent_normed, latent_hat, latent_istd, latent_gain
        )
        grad_latent_one = (grad_mid + grad_latent_in).astype(jnp.bfloat16)
        carry = (
            down_acc,
            up_acc,
            output_acc,
            keyval_acc,
            query_acc,
            mg_acc + mg_part,
            mb_acc + mb_part,
            lg_acc + lg_part,
            lb_acc + lb_part,
            fg_acc + fg_part,
            fb_acc + fb_part,
            time_acc,
        )
        return (carry, (out_one, grad_media_in.astype(jnp.bfloat16), grad_latent_one))

    ff_local = up_weight.shape[1]
    vector_zero = jnp.zeros((width,), jnp.float32)
    start = (
        jnp.zeros((ff_local, width), jnp.float32),
        jnp.zeros((width, ff_local), jnp.float32),
        jnp.zeros((cols, width), jnp.float32),
        jnp.zeros((width, 2 * cols), jnp.float32),
        jnp.zeros((width, cols), jnp.float32),
        vector_zero,
        vector_zero,
        vector_zero,
        vector_zero,
        vector_zero,
        vector_zero,
        jnp.zeros((FRAMES_MAX, width), jnp.float32),
    )
    totals, stacked = lax.scan(item_step, start, (media_feats, latents, valid_tok, cotangent))
    (
        down_acc,
        up_acc,
        output_acc,
        keyval_acc,
        query_acc,
        mg_acc,
        mb_acc,
        lg_acc,
        lb_acc,
        fg_acc,
        fb_acc,
        time_acc,
    ) = totals
    out_latents, grad_media, grad_latents = stacked
    up_sum, down_sum, query_sum, keyval_sum, output_sum = (
        lax.psum_scatter(
            up_acc.astype(jnp.bfloat16), "wide", scatter_dimension=0, tiled=True
        ).astype(jnp.float32),
        lax.psum_scatter(
            down_acc.astype(jnp.bfloat16), "wide", scatter_dimension=1, tiled=True
        ).astype(jnp.float32),
        lax.psum_scatter(
            query_acc.astype(jnp.bfloat16), "wide", scatter_dimension=0, tiled=True
        ).astype(jnp.float32),
        lax.psum_scatter(
            keyval_acc.reshape(width, 2, cols).astype(jnp.bfloat16),
            "wide",
            scatter_dimension=0,
            tiled=True,
        ).astype(jnp.float32),
        lax.psum_scatter(
            output_acc.astype(jnp.bfloat16), "wide", scatter_dimension=1, tiled=True
        ).astype(jnp.float32),
    )
    mg_sum, mb_sum, lg_sum, lb_sum, fg_sum, fb_sum, time_sum = (
        lax.psum_scatter(mg_acc, ("wide", "narrow"), scatter_dimension=0, tiled=True),
        lax.psum_scatter(mb_acc, ("wide", "narrow"), scatter_dimension=0, tiled=True),
        lax.psum_scatter(lg_acc, ("wide", "narrow"), scatter_dimension=0, tiled=True),
        lax.psum_scatter(lb_acc, ("wide", "narrow"), scatter_dimension=0, tiled=True),
        lax.psum_scatter(fg_acc, ("wide", "narrow"), scatter_dimension=0, tiled=True),
        lax.psum_scatter(fb_acc, ("wide", "narrow"), scatter_dimension=0, tiled=True),
        lax.psum_scatter(time_acc, ("wide", "narrow"), scatter_dimension=1, tiled=True),
    )
    return (
        out_latents,
        grad_media,
        grad_latents,
        time_sum,
        mg_sum,
        mb_sum,
        lg_sum,
        lb_sum,
        fg_sum,
        fb_sum,
        query_sum,
        keyval_sum,
        output_sum,
        up_sum,
        down_sum,
    )


def solution(mesh):
    placed = (
        P("wide", "narrow", None),
        P("wide", "narrow", None),
        P("wide"),
        P("wide", None),
        P(),
        P(),
        P(),
        P(),
        P(),
        P(),
        P(),
        P("wide", "narrow"),
        P("wide", None, "narrow"),
        P("narrow", "wide"),
        P(None, "narrow"),
        P("narrow", None),
        P("wide", "narrow", None),
    )
    return jax.shard_map(
        body,
        mesh=mesh,
        in_specs=placed,
        out_specs=(
            P("wide", "narrow", None),
            P("wide", "narrow", None),
            P("wide", "narrow", None),
            P(None, ("wide", "narrow")),
            P(("wide", "narrow")),
            P(("wide", "narrow")),
            P(("wide", "narrow")),
            P(("wide", "narrow")),
            P(("wide", "narrow")),
            P(("wide", "narrow")),
            P("wide", "narrow"),
            P("wide", None, "narrow"),
            P("narrow", "wide"),
            P("wide", "narrow"),
            P("narrow", "wide"),
        ),
        check_vma=False,
    )
```

profile of v0, /device:TPU:0, one launch (start us, length us, event | category | flops | bytes accessed | tf_op | source)
XLA Modules:
  0.0 941.4 jit_solution(12498868731809088327)
XLA Ops:
  15.3 6.9 all_gather.36
  23.6 30.5 %all-gather.12.cloned.1.call-done = bf16[1536,384]{1,0:T(8,128)(2,1)} async-done(((bf16[192,384]{1,0:T(8,128)(2,1)}), bf16[1536,384]{1,0:T(8,128)(2,1)}) %all-gather.12.cloned.1.call-update) | async-done | bytes 1179664 | tf_op jit(solution)/shard_map/all_gather | solution.py:77
  55.8 51.6 %all-gather.10.cloned.1.call-done = bf16[1536,2,384]{2,0,1:T(8,128)(2,1)} async-done(((bf16[192,2,384]{2,0,1:T(8,128)(2,1)}), bf16[1536,2,384]{2,0,1:T(8,128)(2,1)}) %all-gather.10.cloned.1.call-update) | async-done | bytes 2359312 | tf_op jit(solution)/shard_map/all_gather | solution.py:78
  107.4 4.3 copy.117
  111.7 42.8 %all-gather.8.cloned.1.call-done = bf16[2048,1536]{1,0:T(8,128)(2,1)} async-done(((bf16[512,1536]{1,0:T(8,128)(2,1)}), bf16[2048,1536]{1,0:T(8,128)(2,1)}) %all-gather.8.cloned.1.call-update) | async-done | bytes 6291472 | tf_op jit(solution)/shard_map/while/body/eval_jaxpr/all_gather | solution.py:115
  157.9 5.5 convolution_convert_fusion.2
  181.3 16.3 %all-gather.14.cloned.1.call-done = bf16[384,1536]{0,1:T(8,128)(2,1)} async-done(((bf16[384,192]{0,1:T(8,128)(2,1)}), bf16[384,1536]{0,1:T(8,128)(2,1)}) %all-gather.14.cloned.1.call-update) | async-done | bytes 1179664 | tf_op jit(solution)/shard_map/all_gather | solution.py:79
  200.1 7.1 all-gather
  207.2 11.8 %reduce-scatter.11.cloned.1.call-done = bf16[16,1536]{1,0:T(8,128)(2,1)} async-done(((bf16[64,1536]{1,0:T(8,128)(2,1)}), bf16[16,1536]{1,0:T(8,128)(2,1)}) %reduce-scatter.11.cloned.1.call-update) | async-done | bytes 49168 | tf_op jit(solution)/shard_map/while/body/eval_jaxpr/reduce_scatter | solution.py:146
  221.9 5.6 all_gather.40
  231.5 4.0 fusion.8
  236.2 4.6 convolution_convert_fusion.7
  241.6 19.1 %reduce-scatter.15.cloned.1.call-done = bf16[16,1536]{1,0:T(8,128)(2,1)} async-done(((bf16[64,1536]{1,0:T(8,128)(2,1)}), bf16[16,1536]{1,0:T(8,128)(2,1)}) %reduce-scatter.15.cloned.1.call-update) | async-done | bytes 49168 | tf_op jit(solution)/shard_map/while/body/eval_jaxpr/reduce_scatter | solution.py:173
  263.2 5.6 all_gather.42
  272.6 22.0 %psum.7 = f32[]{:T(128)} all-reduce(f32[]{:T(128)S(6)} %add.196), channel_id=1, replica_groups=mesh['wide'=8,'narrow'=4] {'wide'}, use_global_device_ids=true, to_apply=%region_14.15 | all-reduce | flops 1 | bytes 8 | tf_op jit(solution)/shard_map/psum | solution.py:73
  295.4 4.2 multiply_reduce_fusion.4
  316.8 10.9 %convolution_convert_fusion.4 = bf16[1536,768]{0,1:T(8,128)(2,1)} fusion(bf16[2112,1536]{1,0:T(8,128)(2,1)} %copy-done.6, bf16[2112,384]{0,1:T(8,128)(2,1)S(1)} %bitcast.160, bf16[2112,384]{0,1:T(8,128)(2,1)S(1)} %bitcast.155), kind=kOutput, calls=%fused_computation.19 | convolution fusion | flops 4990500864 | bytes 12091392 | tf_op jit(solution)/shard_map/while/body/eval_jaxpr/kd,ke->de/dot_general | solution.py:215
  327.7 6.9 copy.135
  338.8 8.7 copy.126
  347.6 4.7 all-to-all-start
  352.3 4.7 convolution_convert_fusion.8
  357.3 31.9 %all-to-all-done = bf16[2048,2,384]{2,1,0:T(2,128)(2,1)} async-done(((bf16[2048,2,384]{2,1,0:T(2,128)(2,1)}), bf16[2048,2,384]{2,1,0:T(2,128)(2,1)}, u32[]{:S(2)}, u32[]{:S(2)}) %all-to-all-start) | async-done | bytes 3145760 | tf_op jit(solution)/shard_map/while/body/eval_jaxpr/all_to_all | solution.py:230
  393.5 10.0 %multiply_reduce_fusion = (f32[1536]{0:T(1024)}, f32[512]{0:T(512)S(1)}, f32[512]{0:T(512)S(1)}, f32[1536]{0:T(1024)}, f32[512,1536]{1,0:T(8,128)S(1)}) fusion(f32[512,1536]{1,0:T(8,128)S(1)} %get-tuple-element.150, f32[512]{0:T(512)S(1)} %add_rsqrt_fusion, f32[512]{0:T(512)S(1)} %broadcast_multiply_fusion.2, f32[1536]{0:T(1024)S(1)} %copy-done.33, ...), kind=kOutput, calls=%fused_computation.23 | convolution fusion | flops 4838912000 | bytes 18900992 | tf_op jit(solution)/shard_map/while/body/eval_jaxpr/rsc,dsc->rd/dot_general | solution.py:233
  413.9 3.9 convolution_convert_fusion
  431.6 31.3 %reduce-scatter.17.cloned.1.call-done = bf16[192,384]{1,0:T(8,128)(2,1)} async-done(((bf16[1536,384]{1,0:T(8,128)(2,1)}), bf16[192,384]{1,0:T(8,128)(2,1)}) %reduce-scatter.17.cloned.1.call-update) | async-done | bytes 147472 | tf_op jit(solution)/shard_map/reduce_scatter | solution.py:306
  464.6 109.4 %all-reduce.11.cloned.1.call-done = bf16[1536,2,384]{2,1,0:T(2,128)(2,1)} async-done(((bf16[1536,2,384]{2,1,0:T(2,128)(2,1)}), bf16[1536,2,384]{2,1,0:T(2,128)(2,1)}) %all-reduce.11.cloned.1.call-update) | async-done | bytes 2359312
  576.0 6.2 convolution_bitcast_fusion.2
  582.3 29.8 %all-gather.18.cloned.1.call-done = bf16[1536,1536]{1,0:T(8,128)(2,1)} async-done(((bf16[1536,384]{1,0:T(8,128)(2,1)}), bf16[1536,1536]{1,0:T(8,128)(2,1)}) %all-gather.18.cloned.1.call-update) | async-done | bytes 4718608 | tf_op jit(solution)/shard_map/all_gather | solution.py:82
  616.0 40.1 %all-reduce.8 = (f32[1536]{0:T(1024)S(1)}, f32[1536]{0:T(1024)S(1)}, f32[1536]{0:T(1024)S(1)}, f32[1536]{0:T(1024)S(1)}, f32[1536]{0:T(1024)S(1)}, /*index=5*/f32[1536]{0:T(1024)S(1)}) all-reduce(f32[1536]{0:T(1024)S(1)} %copy-done.46, f32[1536]{0:T(1024)S(1)} %copy-done.47, ...), channel_id=7, replica_groups=mesh['wide'=8,'narrow'=4] {'wide','narrow'}, use_global_device_ids=true, to_apply=%region_23.24.clone | all-reduce | flops 9216 | bytes 73728
  661.2 74.4 %reduce-scatter.25.cloned.1.call-done = f32[48,8]{1,0:T(8,128)} async-done(((f32[1536,8]{1,0:T(8,128)}), f32[48,8]{1,0:T(8,128)}) %reduce-scatter.25.cloned.1.call-update) | async-done | bytes 1552
  737.0 96.9 %reduce-scatter.21.cloned.1.call-done = bf16[192,1536]{1,0:T(8,128)(2,1)} async-done(((bf16[1536,1536]{1,0:T(8,128)(2,1)}), bf16[192,1536]{1,0:T(8,128)(2,1)}) %reduce-scatter.21.cloned.1.call-update) | async-done | bytes 589840 | tf_op jit(solution)/shard_map/reduce_scatter | solution.py:300
  836.0 96.6 %reduce-scatter.23.cloned.1.call-done = bf16[1536,192]{0,1:T(8,128)(2,1)} async-done(((bf16[1536,1536]{0,1:T(8,128)(2,1)}), bf16[1536,192]{0,1:T(8,128)(2,1)}) %reduce-scatter.23.cloned.1.call-update) | async-done | bytes 589840 | tf_op jit(solution)/shard_map/reduce_scatter | solution.py:303
  (234 shorter events, 115.8 us)
Async XLA Ops:
  7.2 46.9 %all-gather.12.cloned.1.call-start = ((), (), s32[]{:S(2)}) async-start(), calls=%async_computation.12 | async-start | bytes 1327104 | tf_op jit(solution)/shard_map/all_gather | solution.py:77
  7.9 99.4 %all-gather.10.cloned.1.call-start = ((), (), s32[]{:S(2)}) async-start(), calls=%async_computation.11 | async-start | bytes 2654208 | tf_op jit(solution)/shard_map/all_gather | solution.py:78
  9.7 144.7 %all-gather.8.cloned.1.call-start = ((), (), s32[]{:S(2)}) async-start(), calls=%async_computation.10 | async-start | bytes 7864320 | tf_op jit(solution)/shard_map/while/body/eval_jaxpr/all_gather | solution.py:115
  14.2 183.4 %all-gather.14.cloned.1.call-start = ((), (), s32[]{:S(2)}) async-start(), calls=%async_computation.13 | async-start | bytes 1327104 | tf_op jit(solution)/shard_map/all_gather | solution.py:79
  14.8 204.2 %reduce-scatter.11.cloned.1.call-start = ((), (), s32[]{:S(2)}) async-start(), calls=%async_computation.14 | async-start | bytes 245760 | tf_op jit(solution)/shard_map/while/body/eval_jaxpr/reduce_scatter | solution.py:146
  23.5 149.4 %copy-start.54 = (pred[2112]{0:T(1024)(128)(4,1)}, pred[2112]{0:T(1024)(128)(4,1)S(1)}, u32[]{:S(2)}) copy-start(pred[2112]{0:T(1024)(128)(4,1)S(1)} %concatenate.18) | copy-start | bytes 6340
  55.8 117.2 %copy-start.27 = (bf16[64,4,96]{2,1,0:T(4,128)(2,1)}, bf16[64,4,96]{2,1,0:T(4,128)(2,1)S(1)}, u32[]{:S(2)}) copy-start(bf16[64,4,96]{2,1,0:T(4,128)(2,1)S(1)} %reshape.235) | copy-start | bytes 147460
  176.6 127.5 %copy-start.57 = (f32[4,64]{1,0:T(4,128)}, f32[4,64]{1,0:T(4,128)S(1)}, u32[]{:S(2)}) copy-start(f32[4,64]{1,0:T(4,128)S(1)} %get-tuple-element.151) | copy-start | bytes 3076
  176.6 44.4 %copy-start.28 = (f32[1536]{0:T(1024)S(1)}, f32[1536]{0:T(1024)}, u32[]{:S(2)}) copy-start(f32[1536]{0:T(1024)} %param.26) | copy-start | bytes 18436
  176.6 44.4 %copy-start.44 = (f32[1536]{0:T(1024)S(1)}, f32[1536]{0:T(1024)}, u32[]{:S(2)}) copy-start(f32[1536]{0:T(1024)} %param.27) | copy-start | bytes 18436
  181.3 50.1 %copy-start.18 = (f32[64,384]{1,0:T(8,128)}, f32[64,384]{1,0:T(8,128)S(1)}, u32[]{:S(2)}) copy-start(f32[64,384]{1,0:T(8,128)S(1)} %reshape.237) | copy-start | bytes 294916
  200.1 60.6 %reduce-scatter.15.cloned.1.call-start = ((), (), s32[]{:S(2)}) async-start(), calls=%async_computation.16 | async-start | bytes 245760 | tf_op jit(solution)/shard_map/while/body/eval_jaxpr/reduce_scatter | solution.py:173
  220.0 42.3 %copy-start.36 = (f32[16]{0:T(128)}, f32[16]{0:T(128)S(1)}, u32[]{:S(2)}) copy-start(f32[16]{0:T(128)S(1)} %broadcast_multiply_fusion.7) | copy-start | bytes 196
  240.8 54.6 %copy-start.55 = (pred[2112]{0:T(1024)(128)(4,1)S(1)}, pred[2112]{0:T(1024)(128)(4,1)}, u32[]{:S(2)}) copy-start(pred[2112]{0:T(1024)(128)(4,1)} %copy-done.54) | copy-start | bytes 6340
  240.8 152.7 %all-gather.16.cloned.1.call-start = ((), (), s32[]{:S(2)}) async-start(), calls=%async_computation.17 | async-start | bytes 11796480 | tf_op jit(solution)/shard_map/all_gather | solution.py:83
  241.5 188.5 %reduce-scatter.19.cloned.1.call-start = ((), (), s32[]{:S(2)}) async-start(), calls=%async_computation.20 | async-start | bytes 1327104 | tf_op jit(solution)/shard_map/reduce_scatter | solution.py:315
  271.9 191.0 %reduce-scatter.17.cloned.1.call-start = ((), (), s32[]{:S(2)}) async-start(), calls=%async_computation.19 | async-start | bytes 1327104 | tf_op jit(solution)/shard_map/reduce_scatter | solution.py:306
  311.9 262.1 %all-reduce.11.cloned.1.call-start = ((), (), s32[]{:S(2)}) async-start(), calls=%async_computation.24 | async-start | bytes 4718592
  334.6 277.5 %all-gather.18.cloned.1.call-start = ((), (), s32[]{:S(2)}) async-start(), calls=%async_computation.18 | async-start | bytes 5898240 | tf_op jit(solution)/shard_map/all_gather | solution.py:82
  347.6 41.7 %all-to-all-start = ((bf16[2048,2,384]{2,1,0:T(2,128)(2,1)}), bf16[2048,2,384]{2,1,0:T(2,128)(2,1)}, u32[]{:S(2)}, u32[]{:S(2)}) async-start(bf16[2048,2,384]{2,1,0:T(2,128)(2,1)} %copy.126), calls=%async_computation.3 | async-start | bytes 6291456 | tf_op jit(solution)/shard_map/while/body/eval_jaxpr/all_to_all | solution.py:230
  352.3 307.3 %reduce-scatter.13.cloned.1.call-start = ((), (), s32[]{:S(2)}) async-start(), calls=%async_computation.15 | async-start | bytes 245760 | tf_op jit(solution)/shard_map/while/body/eval_jaxpr/reduce_scatter | solution.py:158
  357.0 378.5 %reduce-scatter.25.cloned.1.call-start = ((), (), s32[]{:S(2)}) async-start(), calls=%async_computation.23 | async-start | bytes 811008
  409.3 424.6 %reduce-scatter.21.cloned.1.call-start = ((), (), s32[]{:S(2)}) async-start(), calls=%async_computation.21 | async-start | bytes 5308416 | tf_op jit(solution)/shard_map/reduce_scatter | solution.py:300
  412.9 519.8 %reduce-scatter.23.cloned.1.call-start = ((), (), s32[]{:S(2)}) async-start(), calls=%async_computation.22 | async-start | bytes 5308416 | tf_op jit(solution)/shard_map/reduce_scatter | solution.py:303
  421.3 8.6 all-to-all-start.1
  582.2 77.3 %copy-start.24 = (bf16[16,1536]{1,0:T(8,128)(2,1)S(1)}, bf16[16,1536]{1,0:T(8,128)(2,1)}, u32[]{:S(2)}) copy-start(bf16[16,1536]{1,0:T(8,128)(2,1)} %reduce-scatter.15.cloned.1.call-done) | copy-start | bytes 147460
  582.2 77.3 %copy-start.26 = (bf16[1,16,1536]{2,1,0:T(8,128)(2,1)S(1)}, bf16[1,16,1536]{2,1,0:T(8,128)(2,1)}, u32[]{:S(2)}) copy-start(bf16[1,16,1536]{2,1,0:T(8,128)(2,1)} %param.33) | copy-start | bytes 147460
  582.3 77.3 %copy-start.37 = (f32[16]{0:T(128)S(1)}, f32[16]{0:T(128)}, u32[]{:S(2)}) copy-start(f32[16]{0:T(128)} %copy-done.36) | copy-start | bytes 196
  582.3 77.3 %copy-start.42 = (f32[16]{0:T(128)S(1)}, f32[16]{0:T(128)}, u32[]{:S(2)}) copy-start(f32[16]{0:T(128)} %copy-done.41) | copy-start | bytes 196
  582.3 77.3 %copy-start.51 = (f32[16]{0:T(128)S(1)}, f32[16]{0:T(128)}, u32[]{:S(2)}) copy-start(f32[16]{0:T(128)} %copy-done.50) | copy-start | bytes 196
  582.3 77.3 %copy-start.53 = (f32[16]{0:T(128)S(1)}, f32[16]{0:T(128)}, u32[]{:S(2)}) copy-start(f32[16]{0:T(128)} %copy-done.52) | copy-start | bytes 196
  612.1 322.7 %copy-start.1 = (bf16[8,1536]{1,0:T(8,128)(2,1)S(1)}, bf16[8,1536]{1,0:T(8,128)(2,1)}, u32[]{:S(2)}) copy-start(bf16[8,1536]{1,0:T(8,128)(2,1)} %param.21) | copy-start | bytes 73732
  (44 other events, 471.9 us)
Sparse Core Ops, SparseCore 0:
  10.2 43.8 all-gather.11
  56.8 50.4 all-gather.9
  109.5 44.8 all-gather.7
  156.5 41.1 all-gather.13
  200.5 18.4 reduce-scatter.10
  240.9 19.7 reduce-scatter.14
  262.3 64.0 all-gather.15
  330.4 64.8 reduce-scatter.18
  399.2 63.7 reduce-scatter.16
  466.4 107.5 all-reduce.10
  575.6 36.5 all-gather.17
  614.4 19.8 reduce-scatter.12
  639.4 96.1 reduce-scatter.24
  739.1 94.7 reduce-scatter.20
  837.3 95.2 reduce-scatter.22
where the time goes:
time: 944 us; the launch traced here: 941 us
  waiting for transfers between devices  649 us (69%)
  matrix products  95.8 us (10%)
  blocking collectives  87.2 us (9%)
  local copies, waits for them, and re-layouts  54.7 us (6%)
  other arithmetic  28.2 us (3%)
  between operations  17.4 us (2%)
    unnamed x17, waiting for transfers between devices  187 us
    reduce_scatter x1, waiting for transfers between devices, body(): lax.psum_scatter(up_acc.astype(jnp.bfloat16), 'wide', scatter_dimension=0...  96.9 us
    reduce_scatter x1, waiting for transfers between devices, body(): lax.psum_scatter(down_acc.astype(jnp.bfloat16), 'wide', scatter_dimension...  96.6 us
    all_gather x1, waiting for transfers between devices, body(): lax.all_gather(keyval_weight, 'wide', axis=0, tiled=True)  51.6 us
    all_gather x1, waiting for transfers between devices, item_step(): lax.all_gather(media_nf.astype(jnp.bfloat16), 'narrow', axis=0, tiled=True)  42.8 us
    unnamed x1, blocking collectives  40.1 us
    all_to_all x1, waiting for transfers between devices, item_step(): lax.all_to_all(media_pairs, 'narrow', split_axis=0, concat_axis=2, tiled=...  31.9 us
    reduce_scatter x1, waiting for transfers between devices, body(): lax.psum_scatter(query_acc.astype(jnp.bfloat16), 'wide', scatter_dimensio...  31.3 us
  transfers between devices with their start and end apart: 17, of which 14 were waited for; matrix products, arithmetic and copies ran while one was open for 16% of the time, Pallas kernels for 0%

commit v1 on v0

--- a/solution.py
+++ b/solution.py
@@ -79,7 +79,9 @@
         lax.all_gather(output_weight, "wide", axis=1, tiled=True),
     )
     query_full, keyval_full = (
-        lax.all_gather(query_own, "narrow", axis=1, tiled=True),
+        jnp.concatenate(
+            lax.all_to_all(jnp.stack([query_own] * lax.axis_size("narrow")), "narrow", 0, 0), axis=1
+        ),
         lax.all_gather(keyval_own, "narrow", axis=2, tiled=True),
     )
     keyval_flat = keyval_own.reshape(width, 2 * cols)

time: 944 us -> 905 us (0.959)
  waiting for transfers between devices: 649 us -> 602 us
    all_gather x1 -> x0, waiting for transfers between devices: 29.8 us -> none  [body(): lax.all_gather(query_own, 'narrow', axis=1, tiled=True)]
    unnamed x17 -> x16, waiting for transfers between devices: 187 us -> 177 us
  transfers between devices with their start and end apart: 17 -> 17, of which waited for: 14 -> 13; matrix products, arithmetic and copies ran while one was open for 16% -> 17% of each run, Pallas kernels for 0% -> 0%
where the time goes in v1:
time: 905 us; the launch traced here: 903 us
  waiting for transfers between devices  602 us (67%)
  matrix products  95.2 us (11%)
  blocking collectives  87.4 us (10%)
  local copies, waits for them, and re-layouts  58 us (6%)
  other arithmetic  28.3 us (3%)
  between operations  17.4 us (2%)
  starting transfers between devices  14.2 us (2%)
    unnamed x16, waiting for transfers between devices  177 us
    reduce_scatter x1, waiting for transfers between devices, body(): lax.psum_scatter(up_acc.astype(jnp.bfloat16), 'wide', scatter_dimension=0...  97 us
    reduce_scatter x1, waiting for transfers between devices, body(): lax.psum_scatter(down_acc.astype(jnp.bfloat16), 'wide', scatter_dimension...  96.6 us
    all_gather x1, waiting for transfers between devices, body(): lax.all_gather(keyval_weight, 'wide', axis=0, tiled=True)  51.6 us
    all_gather x1, waiting for transfers between devices, item_step(): lax.all_gather(media_nf.astype(jnp.bfloat16), 'narrow', axis=0, tiled=True)  42.8 us
    unnamed x1, blocking collectives  40.3 us
    all_to_all x1, waiting for transfers between devices, item_step(): lax.all_to_all(media_pairs, 'narrow', split_axis=0, concat_axis=2, tiled=...  31.9 us
    all_gather x1, waiting for transfers between devices, body(): lax.all_gather(query_weight, 'wide', axis=0, tiled=True)  30.5 us
  transfers between devices with their start and end apart: 17, of which 13 were waited for; matrix products, arithmetic and copies ran while one was open for 17% of the time, Pallas kernels for 0%

profile of v1, /device:TPU:0, one launch (start us, length us, event | category | flops | bytes accessed | tf_op | source)
XLA Modules:
  0.0 902.7 jit_solution(5357242828063476250)
XLA Ops:
  15.3 6.9 all_gather.33
  23.6 30.5 %all-gather.11.cloned.1.call-done = bf16[1536,384]{1,0:T(8,128)(2,1)} async-done(((bf16[192,384]{1,0:T(8,128)(2,1)}), bf16[1536,384]{1,0:T(8,128)(2,1)}) %all-gather.11.cloned.1.call-update) | async-done | bytes 1179664 | tf_op jit(solution)/shard_map/all_gather | solution.py:77
  55.8 51.6 %all-gather.9.cloned.1.call-done = bf16[1536,2,384]{2,0,1:T(8,128)(2,1)} async-done(((bf16[192,2,384]{2,0,1:T(8,128)(2,1)}), bf16[1536,2,384]{2,0,1:T(8,128)(2,1)}) %all-gather.9.cloned.1.call-update) | async-done | bytes 2359312 | tf_op jit(solution)/shard_map/all_gather | solution.py:78
  107.4 4.3 copy.121
  111.7 42.8 %all-gather.7.cloned.1.call-done = bf16[2048,1536]{1,0:T(8,128)(2,1)} async-done(((bf16[512,1536]{1,0:T(8,128)(2,1)}), bf16[2048,1536]{1,0:T(8,128)(2,1)}) %all-gather.7.cloned.1.call-update) | async-done | bytes 6291472 | tf_op jit(solution)/shard_map/while/body/eval_jaxpr/all_gather | solution.py:117
  157.9 5.5 convolution_convert_fusion.2
  181.3 16.3 %all-gather.13.cloned.1.call-done = bf16[384,1536]{0,1:T(8,128)(2,1)} async-done(((bf16[384,192]{0,1:T(8,128)(2,1)}), bf16[384,1536]{0,1:T(8,128)(2,1)}) %all-gather.13.cloned.1.call-update) | async-done | bytes 1179664 | tf_op jit(solution)/shard_map/all_gather | solution.py:79
  200.1 7.1 all-gather
  207.2 11.7 %reduce-scatter.11.cloned.1.call-done = bf16[16,1536]{1,0:T(8,128)(2,1)} async-done(((bf16[64,1536]{1,0:T(8,128)(2,1)}), bf16[16,1536]{1,0:T(8,128)(2,1)}) %reduce-scatter.11.cloned.1.call-update) | async-done | bytes 49168 | tf_op jit(solution)/shard_map/while/body/eval_jaxpr/reduce_scatter | solution.py:148
  221.9 5.6 all_gather.37
  231.5 4.0 fusion.8
  236.2 4.6 convolution_convert_fusion.7
  241.6 19.1 %reduce-scatter.15.cloned.1.call-done = bf16[16,1536]{1,0:T(8,128)(2,1)} async-done(((bf16[64,1536]{1,0:T(8,128)(2,1)}), bf16[16,1536]{1,0:T(8,128)(2,1)}) %reduce-scatter.15.cloned.1.call-update) | async-done | bytes 49168 | tf_op jit(solution)/shard_map/while/body/eval_jaxpr/reduce_scatter | solution.py:175
  263.2 5.6 all_gather.39
  272.6 22.0 %psum.7 = f32[]{:T(128)} all-reduce(f32[]{:T(128)S(6)} %add.196), channel_id=1, replica_groups=mesh['wide'=8,'narrow'=4] {'wide'}, use_global_device_ids=true, to_apply=%region_14.15 | all-reduce | flops 1 | bytes 8 | tf_op jit(solution)/shard_map/psum | solution.py:73
  295.4 4.2 multiply_reduce_fusion.4
  316.8 10.9 %convolution_convert_fusion.4 = bf16[1536,768]{0,1:T(8,128)(2,1)} fusion(bf16[2112,1536]{1,0:T(8,128)(2,1)} %copy-done.6, bf16[2112,384]{0,1:T(8,128)(2,1)S(1)} %bitcast.163, bf16[2112,384]{0,1:T(8,128)(2,1)S(1)} %bitcast.158), kind=kOutput, calls=%fused_computation.19 | convolution fusion | flops 4990500864 | bytes 12091392 | tf_op jit(solution)/shard_map/while/body/eval_jaxpr/kd,ke->de/dot_general | solution.py:217
  327.7 6.9 copy.140
  338.1 8.7 copy.130
  346.9 4.7 all-to-all-start
  351.7 4.7 convolution_convert_fusion.8
  356.7 31.9 %all-to-all-done = bf16[2048,2,384]{2,1,0:T(2,128)(2,1)} async-done(((bf16[2048,2,384]{2,1,0:T(2,128)(2,1)}), bf16[2048,2,384]{2,1,0:T(2,128)(2,1)}, u32[]{:S(2)}, u32[]{:S(2)}) %all-to-all-start) | async-done | bytes 3145760 | tf_op jit(solution)/shard_map/while/body/eval_jaxpr/all_to_all | solution.py:232
  392.9 10.0 %multiply_reduce_fusion = (f32[1536]{0:T(1024)}, f32[512]{0:T(512)S(1)}, f32[512]{0:T(512)S(1)}, f32[1536]{0:T(1024)}, f32[512,1536]{1,0:T(8,128)S(1)}) fusion(f32[512,1536]{1,0:T(8,128)S(1)} %get-tuple-element.150, f32[512]{0:T(512)S(1)} %add_rsqrt_fusion, f32[512]{0:T(512)S(1)} %broadcast_multiply_fusion.2, f32[1536]{0:T(1024)S(1)} %copy-done.34, ...), kind=kOutput, calls=%fused_computation.23 | convolution fusion | flops 4838912000 | bytes 18900992 | tf_op jit(solution)/shard_map/while/body/eval_jaxpr/rsc,dsc->rd/dot_general | solution.py:235
  424.8 4.6 all-to-all-done.1
  432.0 5.4 all-to-all-start.2
  440.3 22.7 %reduce-scatter.17.cloned.1.call-done = bf16[192,384]{1,0:T(8,128)(2,1)} async-done(((bf16[1536,384]{1,0:T(8,128)(2,1)}), bf16[192,384]{1,0:T(8,128)(2,1)}) %reduce-scatter.17.cloned.1.call-update) | async-done | bytes 147472 | tf_op jit(solution)/shard_map/reduce_scatter | solution.py:308
  464.6 109.4 %all-reduce.11.cloned.1.call-done = bf16[1536,2,384]{2,1,0:T(2,128)(2,1)} async-done(((bf16[1536,2,384]{2,1,0:T(2,128)(2,1)}), bf16[1536,2,384]{2,1,0:T(2,128)(2,1)}) %all-reduce.11.cloned.1.call-update) | async-done | bytes 2359312
  576.1 6.2 convolution_bitcast_fusion.2
  585.7 40.3 %all-reduce.8 = (f32[1536]{0:T(1024)S(1)}, f32[1536]{0:T(1024)S(1)}, f32[1536]{0:T(1024)S(1)}, f32[1536]{0:T(1024)S(1)}, f32[1536]{0:T(1024)S(1)}, /*index=5*/f32[1536]{0:T(1024)S(1)}) all-reduce(f32[1536]{0:T(1024)S(1)} %copy-done.47, f32[1536]{0:T(1024)S(1)} %copy-done.48, ...), channel_id=7, replica_groups=mesh['wide'=8,'narrow'=4] {'wide','narrow'}, use_global_device_ids=true, to_apply=%region_23.24.clone | all-reduce | flops 9216 | bytes 73728
  631.1 65.7 %reduce-scatter.25.cloned.1.call-done = f32[48,8]{1,0:T(8,128)} async-done(((f32[1536,8]{1,0:T(8,128)}), f32[48,8]{1,0:T(8,128)}) %reduce-scatter.25.cloned.1.call-update) | async-done | bytes 1552
  698.2 97.0 %reduce-scatter.21.cloned.1.call-done = bf16[192,1536]{1,0:T(8,128)(2,1)} async-done(((bf16[1536,1536]{1,0:T(8,128)(2,1)}), bf16[192,1536]{1,0:T(8,128)(2,1)}) %reduce-scatter.21.cloned.1.call-update) | async-done | bytes 589840 | tf_op jit(solution)/shard_map/reduce_scatter | solution.py:302
  797.4 96.6 %reduce-scatter.23.cloned.1.call-done = bf16[1536,192]{0,1:T(8,128)(2,1)} async-done(((bf16[1536,1536]{0,1:T(8,128)(2,1)}), bf16[1536,192]{0,1:T(8,128)(2,1)}) %reduce-scatter.23.cloned.1.call-update) | async-done | bytes 589840 | tf_op jit(solution)/shard_map/reduce_scatter | solution.py:305
  (237 shorter events, 117.8 us)
Async XLA Ops:
  7.2 46.9 %all-gather.11.cloned.1.call-start = ((), (), s32[]{:S(2)}) async-start(), calls=%async_computation.13 | async-start | bytes 1327104 | tf_op jit(solution)/shard_map/all_gather | solution.py:77
  7.9 99.4 %all-gather.9.cloned.1.call-start = ((), (), s32[]{:S(2)}) async-start(), calls=%async_computation.12 | async-start | bytes 2654208 | tf_op jit(solution)/shard_map/all_gather | solution.py:78
  9.7 144.7 %all-gather.7.cloned.1.call-start = ((), (), s32[]{:S(2)}) async-start(), calls=%async_computation.11 | async-start | bytes 7864320 | tf_op jit(solution)/shard_map/while/body/eval_jaxpr/all_gather | solution.py:117
  14.2 183.4 %all-gather.13.cloned.1.call-start = ((), (), s32[]{:S(2)}) async-start(), calls=%async_computation.14 | async-start | bytes 1327104 | tf_op jit(solution)/shard_map/all_gather | solution.py:79
  14.8 204.2 %reduce-scatter.11.cloned.1.call-start = ((), (), s32[]{:S(2)}) async-start(), calls=%async_computation.15 | async-start | bytes 245760 | tf_op jit(solution)/shard_map/while/body/eval_jaxpr/reduce_scatter | solution.py:148
  23.5 149.4 %copy-start.55 = (pred[2112]{0:T(1024)(128)(4,1)}, pred[2112]{0:T(1024)(128)(4,1)S(1)}, u32[]{:S(2)}) copy-start(pred[2112]{0:T(1024)(128)(4,1)S(1)} %concatenate.18) | copy-start | bytes 6340
  55.8 117.2 %copy-start.28 = (bf16[64,4,96]{2,1,0:T(4,128)(2,1)}, bf16[64,4,96]{2,1,0:T(4,128)(2,1)S(1)}, u32[]{:S(2)}) copy-start(bf16[64,4,96]{2,1,0:T(4,128)(2,1)S(1)} %reshape.243) | copy-start | bytes 147460
  176.6 127.5 %copy-start.58 = (f32[4,64]{1,0:T(4,128)}, f32[4,64]{1,0:T(4,128)S(1)}, u32[]{:S(2)}) copy-start(f32[4,64]{1,0:T(4,128)S(1)} %get-tuple-element.151) | copy-start | bytes 3076
  176.6 44.4 %copy-start.29 = (f32[1536]{0:T(1024)S(1)}, f32[1536]{0:T(1024)}, u32[]{:S(2)}) copy-start(f32[1536]{0:T(1024)} %param.26) | copy-start | bytes 18436
  176.6 44.4 %copy-start.45 = (f32[1536]{0:T(1024)S(1)}, f32[1536]{0:T(1024)}, u32[]{:S(2)}) copy-start(f32[1536]{0:T(1024)} %param.27) | copy-start | bytes 18436
  181.3 50.1 %copy-start.19 = (f32[64,384]{1,0:T(8,128)}, f32[64,384]{1,0:T(8,128)S(1)}, u32[]{:S(2)}) copy-start(f32[64,384]{1,0:T(8,128)S(1)} %reshape.245) | copy-start | bytes 294916
  200.1 60.6 %reduce-scatter.15.cloned.1.call-start = ((), (), s32[]{:S(2)}) async-start(), calls=%async_computation.17 | async-start | bytes 245760 | tf_op jit(solution)/shard_map/while/body/eval_jaxpr/reduce_scatter | solution.py:175
  220.0 42.3 %copy-start.37 = (f32[16]{0:T(128)}, f32[16]{0:T(128)S(1)}, u32[]{:S(2)}) copy-start(f32[16]{0:T(128)S(1)} %broadcast_multiply_fusion.7) | copy-start | bytes 196
  240.7 54.6 %copy-start.56 = (pred[2112]{0:T(1024)(128)(4,1)S(1)}, pred[2112]{0:T(1024)(128)(4,1)}, u32[]{:S(2)}) copy-start(pred[2112]{0:T(1024)(128)(4,1)} %copy-done.55) | copy-start | bytes 6340
  240.8 152.2 %all-gather.15.cloned.1.call-start = ((), (), s32[]{:S(2)}) async-start(), calls=%async_computation.18 | async-start | bytes 11796480 | tf_op jit(solution)/shard_map/all_gather | solution.py:85
  241.5 197.2 %reduce-scatter.19.cloned.1.call-start = ((), (), s32[]{:S(2)}) async-start(), calls=%async_computation.20 | async-start | bytes 1327104 | tf_op jit(solution)/shard_map/reduce_scatter | solution.py:317
  271.9 191.1 %reduce-scatter.17.cloned.1.call-start = ((), (), s32[]{:S(2)}) async-start(), calls=%async_computation.19 | async-start | bytes 1327104 | tf_op jit(solution)/shard_map/reduce_scatter | solution.py:308
  311.9 262.2 %all-reduce.11.cloned.1.call-start = ((), (), s32[]{:S(2)}) async-start(), calls=%async_computation.24 | async-start | bytes 4718592
  346.9 41.7 %all-to-all-start = ((bf16[2048,2,384]{2,1,0:T(2,128)(2,1)}), bf16[2048,2,384]{2,1,0:T(2,128)(2,1)}, u32[]{:S(2)}, u32[]{:S(2)}) async-start(bf16[2048,2,384]{2,1,0:T(2,128)(2,1)} %copy.130), calls=%async_computation.3 | async-start | bytes 6291456 | tf_op jit(solution)/shard_map/while/body/eval_jaxpr/all_to_all | solution.py:232
  351.7 277.9 %reduce-scatter.13.cloned.1.call-start = ((), (), s32[]{:S(2)}) async-start(), calls=%async_computation.16 | async-start | bytes 245760 | tf_op jit(solution)/shard_map/while/body/eval_jaxpr/reduce_scatter | solution.py:160
  356.4 340.4 %reduce-scatter.25.cloned.1.call-start = ((), (), s32[]{:S(2)}) async-start(), calls=%async_computation.23 | async-start | bytes 811008
  408.7 386.5 %reduce-scatter.21.cloned.1.call-start = ((), (), s32[]{:S(2)}) async-start(), calls=%async_computation.21 | async-start | bytes 5308416 | tf_op jit(solution)/shard_map/reduce_scatter | solution.py:302
  412.4 481.6 %reduce-scatter.23.cloned.1.call-start = ((), (), s32[]{:S(2)}) async-start(), calls=%async_computation.22 | async-start | bytes 5308416 | tf_op jit(solution)/shard_map/reduce_scatter | solution.py:305
  420.8 8.6 all-to-all-start.1
  432.0 150.4 %all-to-all-start.2 = ((bf16[4,1536,384]{1,2,0:T(8,128)(2,1)}), bf16[4,1536,384]{1,2,0:T(8,128)(2,1)}, u32[]{:S(2)}, u32[]{:S(2)}) async-start(bf16[4,1536,384]{1,2,0:T(8,128)(2,1)} %stack.2), calls=%async_computation.5 | async-start | bytes 9437184 | tf_op jit(solution)/shard_map/all_to_all | solution.py:83
  582.3 47.2 %copy-start.25 = (bf16[16,1536]{1,0:T(8,128)(2,1)S(1)}, bf16[16,1536]{1,0:T(8,128)(2,1)}, u32[]{:S(2)}) copy-start(bf16[16,1536]{1,0:T(8,128)(2,1)} %reduce-scatter.15.cloned.1.call-done) | copy-start | bytes 147460
  582.3 47.2 %copy-start.27 = (bf16[1,16,1536]{2,1,0:T(8,128)(2,1)S(1)}, bf16[1,16,1536]{2,1,0:T(8,128)(2,1)}, u32[]{:S(2)}) copy-start(bf16[1,16,1536]{2,1,0:T(8,128)(2,1)} %param.33) | copy-start | bytes 147460
  582.4 47.2 %copy-start.38 = (f32[16]{0:T(128)S(1)}, f32[16]{0:T(128)}, u32[]{:S(2)}) copy-start(f32[16]{0:T(128)} %copy-done.37) | copy-start | bytes 196
  582.4 47.2 %copy-start.43 = (f32[16]{0:T(128)S(1)}, f32[16]{0:T(128)}, u32[]{:S(2)}) copy-start(f32[16]{0:T(128)} %copy-done.42) | copy-start | bytes 196
  582.4 47.2 %copy-start.52 = (f32[16]{0:T(128)S(1)}, f32[16]{0:T(128)}, u32[]{:S(2)}) copy-start(f32[16]{0:T(128)} %copy-done.51) | copy-start | bytes 196
  582.4 47.2 %copy-start.54 = (f32[16]{0:T(128)S(1)}, f32[16]{0:T(128)}, u32[]{:S(2)}) copy-start(f32[16]{0:T(128)} %copy-done.53) | copy-start | bytes 196
  582.4 313.8 %copy-start.1 = (bf16[8,1536]{1,0:T(8,128)(2,1)S(1)}, bf16[8,1536]{1,0:T(8,128)(2,1)}, u32[]{:S(2)}) copy-start(bf16[8,1536]{1,0:T(8,128)(2,1)} %param.21) | copy-start | bytes 73732
  (45 other events, 326.3 us)
Sparse Core Ops, SparseCore 0:
  10.2 43.8 all-gather.10
  56.8 50.4 all-gather.8
  109.5 44.8 all-gather.6
  156.5 41.1 all-gather.12
  200.5 18.4 reduce-scatter.10
  240.9 19.7 reduce-scatter.14
  262.3 64.0 all-gather.14
  330.3 64.8 reduce-scatter.18
  399.2 63.7 reduce-scatter.16
  466.4 107.6 all-reduce.10
  576.5 19.1 reduce-scatter.12
  600.7 95.9 reduce-scatter.24
  700.4 94.6 reduce-scatter.20
  798.7 95.2 reduce-scatter.22
